TPU v7x, 256 devices: a whole 4x4x8 slice. The times are simulated.
256 devices in a mesh: dp: 16 (over x_lo, z), tensor: 16 (over y, x_hi, core).
Axes of the slice: x: 4 (x_hi: 2, x_lo: 2; x = x_hi * 2 + x_lo), y: 4, z: 8, core: 2. Of those that a mesh axis runs over, the one named last changes fastest.
Arguments:
- query_rows: bfloat16 [32768, 8192], P('dp', 'tensor'), may hold values from -16 to 16
- key_rows: bfloat16 [32768, 1024], P('dp'), may hold values from -10 to 10
- value_rows: bfloat16 [32768, 1024], P('dp'), may hold values from -600 to 600
- segment_ids: int32 [32768], P('dp'), may hold values from 0 to 127, never falling along the last dimension, each value on 1 to 512 neighbouring positions
- norm_gain: float32 [8192], replicated, may hold values from 0.1 to 1.9
- draft_weight: bfloat16 [8192, 512], P('tensor', 'dp'), may hold values from -0.0625 to 0.0625
- targets: bfloat16 [32768, 512], P(('dp', 'tensor')), may hold values from -6 to 6
Outputs:
- grad_weight: float32 [8192, 512], P('tensor', 'dp')
Inputs may be any that keep to these rules, and one draw needn't show every extreme that they name: `segment_ids`: document ids never fall along the tokens; a document has at most 512 tokens, and one has exactly 512.
All inputs are finite; a program needn't handle non-finite values.
Results may differ from a plain program's by a relative error of at most 0.0015.
Values may be sent and summed in bfloat16 or wider, within the bound.
No kernel may reach another device: no remote copies, remote signals or barrier semaphores. Data moves between devices by JAX's collectives and lax.ppermute only.
A program may use at most 128 MiB of HBM per device.

v0:
```python
import jax
import jax.numpy as jnp
from jax import lax
from jax.sharding import PartitionSpec as P

HEADS = 64
KV_HEADS = 8
HEAD_DIM = 128


def attend_local(query_rows, key_rows, value_rows, segment_ids):
    length = query_rows.shape[0]
    local_heads = query_rows.shape[1] // HEAD_DIM
    group = HEADS // KV_HEADS
    head_count = max(1, local_heads // group)
    repeats = local_heads // head_count
    first = lax.axis_index("tensor") * local_heads // group
    keys_local = lax.dynamic_slice_in_dim(
        key_rows, first * HEAD_DIM, head_count * HEAD_DIM, 1
    ).reshape(length, head_count, HEAD_DIM)
    values_local = lax.dynamic_slice_in_dim(
        value_rows, first * HEAD_DIM, head_count * HEAD_DIM, 1
    ).reshape(length, head_count, HEAD_DIM)
    grouped = query_rows.reshape(length, head_count, repeats, HEAD_DIM)
    width = min(length, 512)
    scale = HEAD_DIM ** (-0.5)
    places = jnp.arange(length, dtype=jnp.int32)

    def one_block(number):
        offset = number * width
        query_block = lax.dynamic_slice_in_dim(grouped, offset, width, 0)
        block_segments = lax.dynamic_slice_in_dim(segment_ids, offset, width, 0)
        block_places = offset + jnp.arange(width, dtype=jnp.int32)
        allowed = (block_segments[:, None] == segment_ids[None, :]) & (
            block_places[:, None] >= places[None, :]
        )
        scores = (
            jnp.einsum(
                "qgrd,kgd->grqk", query_block, keys_local, preferred_element_type=jnp.float32
            )
            * scale
        )
        scores = jnp.where(allowed[None, None], scores, -1e30)
        shifted = jnp.exp(scores - jnp.max(scores, axis=-1, keepdims=True))
        probs = (shifted / jnp.sum(shifted, axis=-1, keepdims=True)).astype(jnp.bfloat16)
        mixed = jnp.einsum(
            "grqk,kgd->qgrd", probs, values_local, preferred_element_type=jnp.float32
        )
        return mixed.astype(jnp.bfloat16).reshape(width, local_heads * HEAD_DIM)

    outputs = lax.map(one_block, jnp.arange(length // width, dtype=jnp.int32))
    return outputs.reshape(length, local_heads * HEAD_DIM)


def loss_derivative(predicted, targets, total_tokens):
    residual = predicted - targets.astype(jnp.float32)
    return (jnp.clip(residual, -1.0, 1.0) / jnp.sqrt(jnp.float32(total_tokens))).astype(
        jnp.bfloat16
    )


def on_device(query_rows, key_rows, value_rows, segment_ids, norm_gain, draft_weight, targets):
    attended = attend_local(query_rows, key_rows, value_rows, segment_ids)
    length = query_rows.shape[0]
    total_tokens = length * lax.axis_size("dp")
    weight_slab = lax.all_gather(draft_weight, "dp", axis=1, tiled=True)
    regrouped = lax.all_to_all(attended, "tensor", split_axis=0, concat_axis=1, tiled=True)
    features = regrouped.astype(jnp.float32)
    mean_square = jnp.mean(features * features, axis=-1, keepdims=True)
    normed = (features * lax.rsqrt(mean_square + 1e-06) * norm_gain[None, :]).astype(jnp.bfloat16)
    picked = normed
    predicted = jnp.dot(
        picked,
        lax.all_gather(weight_slab, "tensor", axis=0, tiled=True),
        preferred_element_type=jnp.float32,
    )
    grad_pred = loss_derivative(predicted, targets, total_tokens)
    picked = normed
    grad_slab = lax.psum_scatter(
        lax.dot_general(
            picked, grad_pred, (((0,), (0,)), ((), ())), preferred_element_type=jnp.float32
        ),
        "tensor",
        scatter_dimension=0,
        tiled=True,
    )
    return lax.psum_scatter(grad_slab, "dp", scatter_dimension=1, tiled=True)


def solution(mesh):
    placed = (
        P("dp", "tensor"),
        P("dp", None),
        P("dp", None),
        P("dp"),
        P(),
        P("tensor", "dp"),
        P(("dp", "tensor"), None),
    )
    return jax.shard_map(
        on_device, mesh=mesh, in_specs=placed, out_specs=P("tensor", "dp"), check_vma=False
    )
```

profile of v0, /device:TPU:8, one launch (start us, length us, event | category | flops | bytes accessed | tf_op | source)
XLA Modules:
  0.0 414.3 jit_solution(10289684197386694751)
XLA Ops:
  6.5 41.8 %all_gather.6 = bf16[512,512]{0,1:T(8,128)(2,1)} all-gather(bf16[512,32]{0,1:T(8,128)(2,1)} %param.14), channel_id=1, replica_groups=mesh['dp'=16,'tensor'=16] {'dp'}, dimensions={1}, use_global_device_ids=true | all-gather | bytes 557056 | tf_op jit(solution)/shard_map/all_gather | solution.py:66
  50.9 2.5 copy.16
  53.4 73.3 %while.11 = (s32[]{:T(128)}, bf16[4,512,512]{2,1,0:T(8,128)(2,1)}, s32[4]{0:T(128)S(1)}, s32[2048]{0:T(1024)S(1)}, bf16[2048,1,4,128]{0,3,2,1:T(8,128)(2,1)}, /*...) while((s32[]{:T(128)}, bf16[4,512,512]{2,1,0:T(8,128)(2,1)}, ...), condition=%wide.region_3.4_spmd.clone, body=%wide.region_0.3_spmd.clone.sunk | while | flops 2201219584 | bytes 58780336 | solution.py:51
  56.0 4.9 %fusion.38 = (f32[4,512]{1,0:T(4,128)S(1)}, f32[512,4,2048]{2,0,1:T(8,128)S(1)}) fusion(pred[512,2048]{1,0:T(8,128)(4,1)S(1)} %fusion.37, bf16[2048,1,128]{2,0,1:T(8,128)(2,1)S(1)} %get-tuple-element.168, bf16[2048,1,4,128]{0,3,2,1:T(8,128)(2,1)} %get-tuple-element.167, s32[]{:T(128)S(6)} %select_n.40), kind=kOutput, calls=%fused_computation.5.clone.1 | convolution fusion | flops 1086322688 | bytes 18882564 | tf_op jit(solution)/shard_map/while/body/eval_jaxpr/qgrd,kgd->grqk/dot_general | solution.py:38
  60.9 4.5 %fusion.39 = f32[4,512]{1,0:T(4,128)S(1)} fusion(f32[512,4,2048]{2,0,1:T(8,128)S(1)} %get-tuple-element.139, f32[4,512]{1,0:T(4,128)S(1)} %get-tuple-element.140, pred[512,2048]{1,0:T(8,128)(4,1)S(1)} %fusion.37), kind=kLoop, calls=%fused_computation.4.clone.1 | loop fusion | flops 16775168 | bytes 17842176 | tf_op jit(solution)/shard_map/while/body/eval_jaxpr/reduce_sum | solution.py:45
  65.4 5.3 %fusion.40 = bf16[4,512,128]{1,2,0:T(8,128)(2,1)S(1)} fusion(f32[4,512]{1,0:T(4,128)S(1)} %fusion.39, f32[4,512]{1,0:T(4,128)S(1)} %get-tuple-element.140, f32[512,4,2048]{2,0,1:T(8,128)S(1)} %get-tuple-element.139, pred[512,2048]{1,0:T(8,128)(4,1)S(1)} %fusion.37, bf16[2048,1,128]{0,2,1:T(8,128)(2,1)S(1)} %get-tuple-element.169), kind=kOutput, calls=%fused_computation.10.clone.1 | convolution fusion | flops 1094975488 | bytes 18890752 | tf_op jit(solution)/shard_map/while/body/eval_jaxpr/grqk,kgd->qgrd/dot_general | solution.py:46
  74.4 4.9 %fusion.38 = (f32[4,512]{1,0:T(4,128)S(1)}, f32[512,4,2048]{2,0,1:T(8,128)S(1)}) fusion(pred[512,2048]{1,0:T(8,128)(4,1)S(1)} %fusion.37, bf16[2048,1,128]{2,0,1:T(8,128)(2,1)S(1)} %get-tuple-element.168, bf16[2048,1,4,128]{0,3,2,1:T(8,128)(2,1)} %get-tuple-element.167, s32[]{:T(128)S(6)} %select_n.40), kind=kOutput, calls=%fused_computation.5.clone.1 | convolution fusion | flops 1086322688 | bytes 18882564 | tf_op jit(solution)/shard_map/while/body/eval_jaxpr/qgrd,kgd->grqk/dot_general | solution.py:38
  79.2 4.5 %fusion.39 = f32[4,512]{1,0:T(4,128)S(1)} fusion(f32[512,4,2048]{2,0,1:T(8,128)S(1)} %get-tuple-element.139, f32[4,512]{1,0:T(4,128)S(1)} %get-tuple-element.140, pred[512,2048]{1,0:T(8,128)(4,1)S(1)} %fusion.37), kind=kLoop, calls=%fused_computation.4.clone.1 | loop fusion | flops 16775168 | bytes 17842176 | tf_op jit(solution)/shard_map/while/body/eval_jaxpr/reduce_sum | solution.py:45
  83.7 5.3 %fusion.40 = bf16[4,512,128]{1,2,0:T(8,128)(2,1)S(1)} fusion(f32[4,512]{1,0:T(4,128)S(1)} %fusion.39, f32[4,512]{1,0:T(4,128)S(1)} %get-tuple-element.140, f32[512,4,2048]{2,0,1:T(8,128)S(1)} %get-tuple-element.139, pred[512,2048]{1,0:T(8,128)(4,1)S(1)} %fusion.37, bf16[2048,1,128]{0,2,1:T(8,128)(2,1)S(1)} %get-tuple-element.169), kind=kOutput, calls=%fused_computation.10.clone.1 | convolution fusion | flops 1094975488 | bytes 18890752 | tf_op jit(solution)/shard_map/while/body/eval_jaxpr/grqk,kgd->qgrd/dot_general | solution.py:46
  92.7 4.9 %fusion.38 = (f32[4,512]{1,0:T(4,128)S(1)}, f32[512,4,2048]{2,0,1:T(8,128)S(1)}) fusion(pred[512,2048]{1,0:T(8,128)(4,1)S(1)} %fusion.37, bf16[2048,1,128]{2,0,1:T(8,128)(2,1)S(1)} %get-tuple-element.168, bf16[2048,1,4,128]{0,3,2,1:T(8,128)(2,1)} %get-tuple-element.167, s32[]{:T(128)S(6)} %select_n.40), kind=kOutput, calls=%fused_computation.5.clone.1 | convolution fusion | flops 1086322688 | bytes 18882564 | tf_op jit(solution)/shard_map/while/body/eval_jaxpr/qgrd,kgd->grqk/dot_general | solution.py:38
  97.6 4.5 %fusion.39 = f32[4,512]{1,0:T(4,128)S(1)} fusion(f32[512,4,2048]{2,0,1:T(8,128)S(1)} %get-tuple-element.139, f32[4,512]{1,0:T(4,128)S(1)} %get-tuple-element.140, pred[512,2048]{1,0:T(8,128)(4,1)S(1)} %fusion.37), kind=kLoop, calls=%fused_computation.4.clone.1 | loop fusion | flops 16775168 | bytes 17842176 | tf_op jit(solution)/shard_map/while/body/eval_jaxpr/reduce_sum | solution.py:45
  102.1 5.3 %fusion.40 = bf16[4,512,128]{1,2,0:T(8,128)(2,1)S(1)} fusion(f32[4,512]{1,0:T(4,128)S(1)} %fusion.39, f32[4,512]{1,0:T(4,128)S(1)} %get-tuple-element.140, f32[512,4,2048]{2,0,1:T(8,128)S(1)} %get-tuple-element.139, pred[512,2048]{1,0:T(8,128)(4,1)S(1)} %fusion.37, bf16[2048,1,128]{0,2,1:T(8,128)(2,1)S(1)} %get-tuple-element.169), kind=kOutput, calls=%fused_computation.10.clone.1 | convolution fusion | flops 1094975488 | bytes 18890752 | tf_op jit(solution)/shard_map/while/body/eval_jaxpr/grqk,kgd->qgrd/dot_general | solution.py:46
  111.0 4.9 %fusion.38 = (f32[4,512]{1,0:T(4,128)S(1)}, f32[512,4,2048]{2,0,1:T(8,128)S(1)}) fusion(pred[512,2048]{1,0:T(8,128)(4,1)S(1)} %fusion.37, bf16[2048,1,128]{2,0,1:T(8,128)(2,1)S(1)} %get-tuple-element.168, bf16[2048,1,4,128]{0,3,2,1:T(8,128)(2,1)} %get-tuple-element.167, s32[]{:T(128)S(6)} %select_n.40), kind=kOutput, calls=%fused_computation.5.clone.1 | convolution fusion | flops 1086322688 | bytes 18882564 | tf_op jit(solution)/shard_map/while/body/eval_jaxpr/qgrd,kgd->grqk/dot_general | solution.py:38
  115.9 4.5 %fusion.39 = f32[4,512]{1,0:T(4,128)S(1)} fusion(f32[512,4,2048]{2,0,1:T(8,128)S(1)} %get-tuple-element.139, f32[4,512]{1,0:T(4,128)S(1)} %get-tuple-element.140, pred[512,2048]{1,0:T(8,128)(4,1)S(1)} %fusion.37), kind=kLoop, calls=%fused_computation.4.clone.1 | loop fusion | flops 16775168 | bytes 17842176 | tf_op jit(solution)/shard_map/while/body/eval_jaxpr/reduce_sum | solution.py:45
  120.4 5.3 %fusion.40 = bf16[4,512,128]{1,2,0:T(8,128)(2,1)S(1)} fusion(f32[4,512]{1,0:T(4,128)S(1)} %fusion.39, f32[4,512]{1,0:T(4,128)S(1)} %get-tuple-element.140, f32[512,4,2048]{2,0,1:T(8,128)S(1)} %get-tuple-element.139, pred[512,2048]{1,0:T(8,128)(4,1)S(1)} %fusion.37, bf16[2048,1,128]{0,2,1:T(8,128)(2,1)S(1)} %get-tuple-element.169), kind=kOutput, calls=%fused_computation.10.clone.1 | convolution fusion | flops 1094975488 | bytes 18890752 | tf_op jit(solution)/shard_map/while/body/eval_jaxpr/grqk,kgd->qgrd/dot_general | solution.py:46
  126.7 33.7 %all_to_all.13 = bf16[16,128,512]{2,1,0:T(8,128)(2,1)S(1)} all-to-all(bf16[16,128,512]{2,1,0:T(8,128)(2,1)} %bitcast.86), channel_id=1, replica_groups=mesh['dp'=16,'tensor'=16] {'tensor'}, dimensions={0} | all-to-all | bytes 4194304 | tf_op jit(solution)/shard_map/all_to_all | solution.py:67
  160.5 2.5 convert_bitcast_fusion
  163.0 5.3 %copy.20 = f32[128,16,512]{0,2,1:T(8,128)} copy(f32[128,16,512]{2,0,1:T(8,128)} %convert_bitcast_fusion) | data formatting | bytes 8388608 | tf_op jit(solution)/shard_map/convert_element_type | solution.py:68
  168.9 2.9 fusion.20
  171.8 6.3 %fusion.23 = bf16[128,512]{1,0:T(8,128)(2,1)S(1)} fusion(bf16[128,8192]{0,1:T(8,128)(2,1)S(1)} %fusion.20, bf16[8192,512]{0,1:T(8,128)(2,1)} %all-gather.2.cloned.1.call-done, bf16[128,512]{1,0:T(8,128)(2,1)S(1)} %copy-done.2), kind=kOutput, calls=%fused_computation.30 | convolution fusion | flops 1074069504 | bytes 10747904 | tf_op jit(solution)/shard_map/dot_general | solution.py:72
  178.1 8.0 %fusion.24 = f32[8192,512]{1,0:T(8,128)} fusion(bf16[128,8192]{0,1:T(8,128)(2,1)S(1)} %fusion.20, bf16[128,512]{1,0:T(8,128)(2,1)S(1)} %fusion.23), kind=kOutput, calls=%fused_computation.34 | convolution fusion | flops 1073741824 | bytes 19005440 | tf_op jit(solution)/shard_map/dot_general | solution.py:80
  186.2 147.4 %reduce-scatter.5.cloned.1.call-done = f32[512,512]{1,0:T(8,128)} async-done(((f32[8192,512]{1,0:T(8,128)}), f32[512,512]{1,0:T(8,128)}) %reduce-scatter.5.cloned.1.call-update) | async-done | bytes 1048592 | tf_op jit(solution)/shard_map/reduce_scatter | solution.py:79
  333.6 2.5 copy.22
  336.1 71.6 %reduce-scatter.7.cloned.1.call-done = f32[32,512]{1,0:T(8,128)} async-done(((f32[512,512]{1,0:T(8,128)}), f32[32,512]{1,0:T(8,128)}) %reduce-scatter.7.cloned.1.call-update) | async-done | bytes 65552
  (46 shorter events, 15.0 us)
Async XLA Ops:
  6.5 44.3 %copy-start = (bf16[2048,512]{1,0:T(8,128)(2,1)S(1)}, bf16[2048,512]{1,0:T(8,128)(2,1)}, u32[]{:S(2)}) copy-start(bf16[2048,512]{1,0:T(8,128)(2,1)} %param.9) | copy-start | bytes 6291460
  6.5 46.9 %copy-start.1 = (s32[2048]{0:T(1024)S(1)}, s32[2048]{0:T(1024)}, u32[]{:S(2)}) copy-start(s32[2048]{0:T(1024)} %param.12) | copy-start | bytes 24580
  6.5 165.2 %all-gather.2.cloned.1.call-start = ((), (), s32[]{:S(2)}) async-start(), calls=%async_computation.3 | async-start | bytes 8912896 | tf_op jit(solution)/shard_map/all_gather | solution.py:74
  48.4 285.2 %reduce-scatter.5.cloned.1.call-start = ((), (), s32[]{:S(2)}) async-start(), calls=%async_computation.4 | async-start | bytes 17825792 | tf_op jit(solution)/shard_map/reduce_scatter | solution.py:79
  163.0 5.9 %copy-start.3 = (f32[8192]{0:T(1024)S(1)}, f32[8192]{0:T(1024)}, u32[]{:S(2)}) copy-start(f32[8192]{0:T(1024)} %param.13) | copy-start | bytes 98308
  168.4 3.4 copy-start.2
  186.1 221.6 %reduce-scatter.7.cloned.1.call-start = ((), (), s32[]{:S(2)}) async-start(), calls=%async_computation.5 | async-start | bytes 1114112
Sparse Core Ops, SparseCore 0:
  48.5 75.7 all-gather.1
  186.2 147.2 reduce-scatter.4
  336.3 71.4 reduce-scatter.6
where the time goes:
time: 415 us; the launch traced here: 414 us
  waiting for transfers between devices  219 us (53%)
  blocking collectives  75.5 us (18%)
  matrix products  55 us (13%)
  other arithmetic  28.6 us (7%)
  local copies, waits for them, and re-layouts  20 us (5%)
  between operations  13.2 us (3%)
    reduce_scatter x1, waiting for transfers between devices, on_device(): lax.psum_scatter(lax.dot_general(picked, grad_pred, (((0,), (0,)), ((), (...  147 us
    unnamed x4, waiting for transfers between devices  71.7 us
    all_gather x1, blocking collectives, on_device(): weight_slab = lax.all_gather(draft_weight, 'dp', axis=1, tiled=True)  41.8 us
    all_to_all x1, blocking collectives, on_device(): lax.all_to_all(attended, 'tensor', split_axis=0, concat_axis=1, tiled=True)  33.7 us
    dot_general x4, matrix products, one_block(): jnp.einsum('grqk,kgd->qgrd', probs, values_local, preferred_element_type=...  21.1 us
    dot_general x4, matrix products, one_block(): jnp.einsum('qgrd,kgd->grqk', query_block, keys_local, preferred_element_t...  19.5 us
    reduce_sum x4, other arithmetic, one_block(): jnp.sum(shifted, axis=-1, keepdims=True)  17.9 us
  transfers between devices with their start and end apart: 3, of which 2 were waited for; matrix products, arithmetic and copies ran while one was open for 21% of the time, Pallas kernels for 0%

commit v1 on v0

--- a/solution.py
+++ b/solution.py
@@ -64,7 +64,12 @@
     length = query_rows.shape[0]
     total_tokens = length * lax.axis_size("dp")
     weight_slab = lax.all_gather(draft_weight, "dp", axis=1, tiled=True)
-    regrouped = lax.all_to_all(attended, "tensor", split_axis=0, concat_axis=1, tiled=True)
+    regrouped = jnp.concatenate(
+        lax.all_to_all(
+            jnp.stack(jnp.split(attended, lax.axis_size("tensor"), axis=0)), "tensor", 0, 0
+        ),
+        axis=1,
+    )
     features = regrouped.astype(jnp.float32)
     mean_square = jnp.mean(features * features, axis=-1, keepdims=True)
     normed = (features * lax.rsqrt(mean_square + 1e-06) * norm_gain[None, :]).astype(jnp.bfloat16)

time: 415 us -> 420 us (1.012)
  matrix products: 55 us -> 60 us
    dot_general x4, matrix products: 21.1 us -> 25.3 us  [one_block(): jnp.einsum('grqk,kgd->qgrd', probs, values_local, preferred_element_type=...]
  transfers between devices with their start and end apart: 3 -> 3, of which waited for: 2 -> 2; matrix products, arithmetic and copies ran while one was open for 21% -> 22% of each run, Pallas kernels for 0% -> 0%
where the time goes in v1:
time: 420 us; the launch traced here: 419 us
  waiting for transfers between devices  219 us (52%)
  blocking collectives  75.2 us (18%)
  matrix products  60 us (14%)
  other arithmetic  28.6 us (7%)
  local copies, waits for them, and re-layouts  20.1 us (5%)
  between operations  13.3 us (3%)
    reduce_scatter x1, waiting for transfers between devices, on_device(): lax.psum_scatter(lax.dot_general(picked, grad_pred, (((0,), (0,)), ((), (...  147 us
    unnamed x4, waiting for transfers between devices  71.8 us
    all_gather x1, blocking collectives, on_device(): weight_slab = lax.all_gather(draft_weight, 'dp', axis=1, tiled=True)  41.7 us
    all_to_all x1, blocking collectives, on_device(): lax.all_to_all(jnp.stack(jnp.split(attended, lax.axis_size('tensor'), axi...  33.5 us
    dot_general x4, matrix products, one_block(): jnp.einsum('grqk,kgd->qgrd', probs, values_local, preferred_element_type=...  25.3 us
    dot_general x4, matrix products, one_block(): jnp.einsum('qgrd,kgd->grqk', query_block, keys_local, preferred_element_t...  20.3 us
    reduce_sum x4, other arithmetic, one_block(): jnp.sum(shifted, axis=-1, keepdims=True)  17.9 us
  transfers between devices with their start and end apart: 3, of which 2 were waited for; matrix products, arithmetic and copies ran while one was open for 22% of the time, Pallas kernels for 0%

profile of v1, /device:TPU:8, one launch (start us, length us, event | category | flops | bytes accessed | tf_op | source)
XLA Modules:
  0.0 419.2 jit_solution(14437266836451340016)
XLA Ops:
  6.5 41.7 %all_gather.6 = bf16[512,512]{0,1:T(8,128)(2,1)} all-gather(bf16[512,32]{0,1:T(8,128)(2,1)} %param.14), channel_id=1, replica_groups=mesh['dp'=16,'tensor'=16] {'dp'}, dimensions={1}, use_global_device_ids=true | all-gather | bytes 557056 | tf_op jit(solution)/shard_map/all_gather | solution.py:66
  52.3 4.0 copy.16
  56.3 74.8 %while.11 = (s32[]{:T(128)}, bf16[4,512,512]{2,1,0:T(8,128)(2,1)S(1)}, s32[4]{0:T(128)S(1)}, s32[2048]{0:T(1024)S(1)}, bf16[2048,1,4,128]{0,3,2,1:T(8,128)(2,1)}...) while((s32[]{:T(128)}, ...), condition=%wide.region_3.4_spmd.clone, body=%wide.region_0.3_spmd.clone.sunk | while | flops 2201219584 | bytes 58779828 | solution.py:51
  58.8 5.1 %fusion.54 = (f32[4,512]{1,0:T(4,128)S(1)}, f32[512,4,2048]{2,0,1:T(8,128)S(1)}) fusion(pred[512,2048]{1,0:T(8,128)(4,1)S(1)} %fusion.53, bf16[2048,1,128]{2,0,1:T(8,128)(2,1)} %get-tuple-element.168, bf16[2048,1,4,128]{0,3,2,1:T(8,128)(2,1)} %get-tuple-element.167, s32[]{:T(128)S(6)} %select_n.40), kind=kOutput, calls=%fused_computation.5.clone.1 | convolution fusion | flops 1086322688 | bytes 18882564 | tf_op jit(solution)/shard_map/while/body/eval_jaxpr/qgrd,kgd->grqk/dot_general | solution.py:38
  63.9 4.5 %fusion.55 = f32[4,512]{1,0:T(4,128)S(1)} fusion(f32[512,4,2048]{2,0,1:T(8,128)S(1)} %get-tuple-element.139, f32[4,512]{1,0:T(4,128)S(1)} %get-tuple-element.140, pred[512,2048]{1,0:T(8,128)(4,1)S(1)} %fusion.53), kind=kLoop, calls=%fused_computation.4.clone.1 | loop fusion | flops 16775168 | bytes 17842176 | tf_op jit(solution)/shard_map/while/body/eval_jaxpr/reduce_sum | solution.py:45
  68.4 6.3 %fusion.56 = bf16[4,512,128]{1,2,0:T(8,128)(2,1)S(1)} fusion(f32[4,512]{1,0:T(4,128)S(1)} %fusion.55, f32[4,512]{1,0:T(4,128)S(1)} %get-tuple-element.140, f32[512,4,2048]{2,0,1:T(8,128)S(1)} %get-tuple-element.139, pred[512,2048]{1,0:T(8,128)(4,1)S(1)} %fusion.53, bf16[2048,1,128]{0,2,1:T(8,128)(2,1)} %get-tuple-element.169), kind=kOutput, calls=%fused_computation.10.clone.1 | convolution fusion | flops 1094975488 | bytes 18890752 | tf_op jit(solution)/shard_map/while/body/eval_jaxpr/grqk,kgd->qgrd/dot_general | solution.py:46
  77.5 5.1 %fusion.54 = (f32[4,512]{1,0:T(4,128)S(1)}, f32[512,4,2048]{2,0,1:T(8,128)S(1)}) fusion(pred[512,2048]{1,0:T(8,128)(4,1)S(1)} %fusion.53, bf16[2048,1,128]{2,0,1:T(8,128)(2,1)} %get-tuple-element.168, bf16[2048,1,4,128]{0,3,2,1:T(8,128)(2,1)} %get-tuple-element.167, s32[]{:T(128)S(6)} %select_n.40), kind=kOutput, calls=%fused_computation.5.clone.1 | convolution fusion | flops 1086322688 | bytes 18882564 | tf_op jit(solution)/shard_map/while/body/eval_jaxpr/qgrd,kgd->grqk/dot_general | solution.py:38
  82.6 4.5 %fusion.55 = f32[4,512]{1,0:T(4,128)S(1)} fusion(f32[512,4,2048]{2,0,1:T(8,128)S(1)} %get-tuple-element.139, f32[4,512]{1,0:T(4,128)S(1)} %get-tuple-element.140, pred[512,2048]{1,0:T(8,128)(4,1)S(1)} %fusion.53), kind=kLoop, calls=%fused_computation.4.clone.1 | loop fusion | flops 16775168 | bytes 17842176 | tf_op jit(solution)/shard_map/while/body/eval_jaxpr/reduce_sum | solution.py:45
  87.1 6.3 %fusion.56 = bf16[4,512,128]{1,2,0:T(8,128)(2,1)S(1)} fusion(f32[4,512]{1,0:T(4,128)S(1)} %fusion.55, f32[4,512]{1,0:T(4,128)S(1)} %get-tuple-element.140, f32[512,4,2048]{2,0,1:T(8,128)S(1)} %get-tuple-element.139, pred[512,2048]{1,0:T(8,128)(4,1)S(1)} %fusion.53, bf16[2048,1,128]{0,2,1:T(8,128)(2,1)} %get-tuple-element.169), kind=kOutput, calls=%fused_computation.10.clone.1 | convolution fusion | flops 1094975488 | bytes 18890752 | tf_op jit(solution)/shard_map/while/body/eval_jaxpr/grqk,kgd->qgrd/dot_general | solution.py:46
  96.2 5.1 %fusion.54 = (f32[4,512]{1,0:T(4,128)S(1)}, f32[512,4,2048]{2,0,1:T(8,128)S(1)}) fusion(pred[512,2048]{1,0:T(8,128)(4,1)S(1)} %fusion.53, bf16[2048,1,128]{2,0,1:T(8,128)(2,1)} %get-tuple-element.168, bf16[2048,1,4,128]{0,3,2,1:T(8,128)(2,1)} %get-tuple-element.167, s32[]{:T(128)S(6)} %select_n.40), kind=kOutput, calls=%fused_computation.5.clone.1 | convolution fusion | flops 1086322688 | bytes 18882564 | tf_op jit(solution)/shard_map/while/body/eval_jaxpr/qgrd,kgd->grqk/dot_general | solution.py:38
  101.3 4.5 %fusion.55 = f32[4,512]{1,0:T(4,128)S(1)} fusion(f32[512,4,2048]{2,0,1:T(8,128)S(1)} %get-tuple-element.139, f32[4,512]{1,0:T(4,128)S(1)} %get-tuple-element.140, pred[512,2048]{1,0:T(8,128)(4,1)S(1)} %fusion.53), kind=kLoop, calls=%fused_computation.4.clone.1 | loop fusion | flops 16775168 | bytes 17842176 | tf_op jit(solution)/shard_map/while/body/eval_jaxpr/reduce_sum | solution.py:45
  105.8 6.3 %fusion.56 = bf16[4,512,128]{1,2,0:T(8,128)(2,1)S(1)} fusion(f32[4,512]{1,0:T(4,128)S(1)} %fusion.55, f32[4,512]{1,0:T(4,128)S(1)} %get-tuple-element.140, f32[512,4,2048]{2,0,1:T(8,128)S(1)} %get-tuple-element.139, pred[512,2048]{1,0:T(8,128)(4,1)S(1)} %fusion.53, bf16[2048,1,128]{0,2,1:T(8,128)(2,1)} %get-tuple-element.169), kind=kOutput, calls=%fused_computation.10.clone.1 | convolution fusion | flops 1094975488 | bytes 18890752 | tf_op jit(solution)/shard_map/while/body/eval_jaxpr/grqk,kgd->qgrd/dot_general | solution.py:46
  114.9 5.1 %fusion.54 = (f32[4,512]{1,0:T(4,128)S(1)}, f32[512,4,2048]{2,0,1:T(8,128)S(1)}) fusion(pred[512,2048]{1,0:T(8,128)(4,1)S(1)} %fusion.53, bf16[2048,1,128]{2,0,1:T(8,128)(2,1)} %get-tuple-element.168, bf16[2048,1,4,128]{0,3,2,1:T(8,128)(2,1)} %get-tuple-element.167, s32[]{:T(128)S(6)} %select_n.40), kind=kOutput, calls=%fused_computation.5.clone.1 | convolution fusion | flops 1086322688 | bytes 18882564 | tf_op jit(solution)/shard_map/while/body/eval_jaxpr/qgrd,kgd->grqk/dot_general | solution.py:38
  120.0 4.5 %fusion.55 = f32[4,512]{1,0:T(4,128)S(1)} fusion(f32[512,4,2048]{2,0,1:T(8,128)S(1)} %get-tuple-element.139, f32[4,512]{1,0:T(4,128)S(1)} %get-tuple-element.140, pred[512,2048]{1,0:T(8,128)(4,1)S(1)} %fusion.53), kind=kLoop, calls=%fused_computation.4.clone.1 | loop fusion | flops 16775168 | bytes 17842176 | tf_op jit(solution)/shard_map/while/body/eval_jaxpr/reduce_sum | solution.py:45
  124.5 6.3 %fusion.56 = bf16[4,512,128]{1,2,0:T(8,128)(2,1)S(1)} fusion(f32[4,512]{1,0:T(4,128)S(1)} %fusion.55, f32[4,512]{1,0:T(4,128)S(1)} %get-tuple-element.140, f32[512,4,2048]{2,0,1:T(8,128)S(1)} %get-tuple-element.139, pred[512,2048]{1,0:T(8,128)(4,1)S(1)} %fusion.53, bf16[2048,1,128]{0,2,1:T(8,128)(2,1)} %get-tuple-element.169), kind=kOutput, calls=%fused_computation.10.clone.1 | convolution fusion | flops 1094975488 | bytes 18890752 | tf_op jit(solution)/shard_map/while/body/eval_jaxpr/grqk,kgd->qgrd/dot_general | solution.py:46
  131.4 33.5 %all_to_all.5 = bf16[16,128,512]{2,1,0:T(8,128)(2,1)S(1)} all-to-all(bf16[16,128,512]{2,1,0:T(8,128)(2,1)S(1)} %fusion.24), channel_id=1, replica_groups=mesh['dp'=16,'tensor'=16] {'tensor'}, dimensions={0} | all-to-all | bytes 4194304 | tf_op jit(solution)/shard_map/all_to_all | solution.py:68
  165.0 2.5 convert_bitcast_fusion
  167.5 5.3 %copy.20 = f32[128,16,512]{0,2,1:T(8,128)} copy(f32[128,16,512]{2,0,1:T(8,128)} %convert_bitcast_fusion) | data formatting | bytes 8388608 | tf_op jit(solution)/shard_map/convert_element_type | solution.py:73
  173.6 2.9 fusion.20
  176.5 6.3 %fusion.23 = bf16[128,512]{1,0:T(8,128)(2,1)S(1)} fusion(bf16[128,8192]{0,1:T(8,128)(2,1)S(1)} %fusion.20, bf16[8192,512]{0,1:T(8,128)(2,1)} %all-gather.2.cloned.1.call-done, bf16[128,512]{1,0:T(8,128)(2,1)S(1)} %copy-done.1), kind=kOutput, calls=%fused_computation.30 | convolution fusion | flops 1074069504 | bytes 10747904 | tf_op jit(solution)/shard_map/dot_general | solution.py:77
  182.8 8.0 %fusion.40 = f32[8192,512]{1,0:T(8,128)} fusion(bf16[128,8192]{0,1:T(8,128)(2,1)S(1)} %fusion.20, bf16[128,512]{1,0:T(8,128)(2,1)S(1)} %fusion.23), kind=kOutput, calls=%fused_computation.66 | convolution fusion | flops 1073741824 | bytes 19005440 | tf_op jit(solution)/shard_map/dot_general | solution.py:85
  191.0 147.5 %reduce-scatter.5.cloned.1.call-done = f32[512,512]{1,0:T(8,128)} async-done(((f32[8192,512]{1,0:T(8,128)}), f32[512,512]{1,0:T(8,128)}) %reduce-scatter.5.cloned.1.call-update) | async-done | bytes 1048592 | tf_op jit(solution)/shard_map/reduce_scatter | solution.py:84
  338.4 2.5 copy.22
  341.0 71.7 %reduce-scatter.7.cloned.1.call-done = f32[32,512]{1,0:T(8,128)} async-done(((f32[512,512]{1,0:T(8,128)}), f32[32,512]{1,0:T(8,128)}) %reduce-scatter.7.cloned.1.call-update) | async-done | bytes 65552
  (60 shorter events, 13.7 us)
Async XLA Ops:
  6.5 170.0 %all-gather.2.cloned.1.call-start = ((), (), s32[]{:S(2)}) async-start(), calls=%async_computation.3 | async-start | bytes 8912896 | tf_op jit(solution)/shard_map/all_gather | solution.py:79
  48.2 290.2 %reduce-scatter.5.cloned.1.call-start = ((), (), s32[]{:S(2)}) async-start(), calls=%async_computation.4 | async-start | bytes 17825792 | tf_op jit(solution)/shard_map/reduce_scatter | solution.py:84
  52.3 4.0 copy-start
  172.9 0.8 copy-start.2
  173.6 2.9 copy-start.1
  190.9 221.8 %reduce-scatter.7.cloned.1.call-start = ((), (), s32[]{:S(2)}) async-start(), calls=%async_computation.5 | async-start | bytes 1114112
Sparse Core Ops, SparseCore 0:
  48.4 75.7 all-gather.1
  191.0 147.3 reduce-scatter.4
  341.1 71.5 reduce-scatter.6
